TPU v7x, 128 devices: a whole 4x4x4 slice. The times are simulated.
128 devices in a mesh: sx: 16 (over y, x_lo, core), sy: 8 (over z, x_hi).
Axes of the slice: x: 4 (x_hi: 2, x_lo: 2; x = x_hi * 2 + x_lo), y: 4, z: 4, core: 2. Of those that a mesh axis runs over, the one named last changes fastest.
Arguments:
- adjoint_loads: float32 [16, 16, 2, 288, 128], P('sx', 'sy'), may hold values from -6 to 6
- dual_taut: bfloat16 [16, 16, 1152, 1152], P('sx', 'sy'), may hold values from -1 to 2
- dual_wrinkle: bfloat16 [16, 16, 1152, 1152], P('sx', 'sy'), may hold values from -1 to 2
- dirichlet_taut: bfloat16 [16, 16, 1152, 1152], P('sx', 'sy'), may hold values from -1 to 2
- dirichlet_wrinkle: bfloat16 [16, 16, 1152, 1152], P('sx', 'sy'), may hold values from -1 to 2
- coupling: bfloat16 [16, 16, 12, 1152], P('sx', 'sy'), may hold values from -0.25 to 0.25
- coarse_inverse: bfloat16 [896, 896], P('sx', 'sy'), may hold values from -1 to 2
- wrinkled: int32 [16, 16], P('sx', 'sy'), may hold values 0 or 1
- edge_lengths: int32 [16, 16, 2], P('sx', 'sy'), may hold values from 144 to 288
- corner_map: int32 [16, 16, 12], P('sx', 'sy'), may hold values from 0 to 895, as said below
Outputs:
- multipliers: float32 [16, 16, 2, 288, 128], P('sx', 'sy')
- preconditioned: float32 [16, 16, 2, 288, 128], P('sx', 'sy')
Inputs may be any that keep to these rules, and one draw needn't show every extreme that they name: `corner_map`: each subdomain names 12 distinct coarse indices, three for each of its four grid corners; subdomains that meet at a grid corner name the same three indices for it; distinct grid corners name distinct indices.
All inputs are finite; a program needn't handle non-finite values. No bound on the sum of `wrinkled` on one device may be relied on, other than what follows from the above.
Results may differ from a plain program's by a relative error of at most 0.012.
Values may be sent and summed in bfloat16 or wider, within the bound.
No kernel may reach another device: no remote copies, remote signals or barrier semaphores. Data moves between devices by JAX's collectives and lax.ppermute only.
A program may use at most 64 MiB of HBM per device.

v0:
```python
import functools

import jax
import jax.numpy as jnp
from jax import lax
from jax.experimental import pallas as pl
from jax.experimental.pallas import tpu as pltpu
from jax.sharding import PartitionSpec as P


CORNERS = 12
SLOT = 16
LANES = 128
LEN_ROWS = 16
PRODUCT_VMEM = 50_000_000
SMALL_VMEM = 16 << 20
EAST, SOUTH, WEST, NORTH = 0, 1, 2, 3
step_sizes = (0.55, 0.75)
momenta = (0.0, 0.15)


F32 = jnp.float32
BF16 = jnp.bfloat16


def shifted(shard, axis, by):
    peers = lax.axis_size(axis)
    return lax.ppermute(shard, axis, [(i, (i + by) % peers) for i in range(peers)])


def copies_of_all(shard, axis):
    peers = lax.axis_size(axis)
    return lax.all_to_all(
        jnp.broadcast_to(shard[None], (peers, *shard.shape)), axis, 0, 0, tiled=True
    )


def exchanged(outgoing):
    east, west, south, north = outgoing
    from_east = None if west is None else shifted(west, "sy", -1)
    from_west = None if east is None else shifted(east, "sy", 1)
    from_south = None if north is None else shifted(north, "sx", -1)
    from_north = None if south is None else shifted(south, "sx", 1)
    return from_east, from_west, from_south, from_north


def dot(a, b, contract=((1,), (0,))):
    return lax.dot_general(a, b, (contract, ((), ())), preferred_element_type=F32)


def below(limit_rows, rows):
    return lax.broadcasted_iota(jnp.int32, (rows, LANES), 0).astype(F32) < limit_rows


VMEM = pl.BlockSpec(memory_space=pltpu.VMEM)
SMEM = pl.BlockSpec(memory_space=pltpu.SMEM)
HBM = pl.BlockSpec(memory_space=pltpu.HBM)


def loads_of(taut, wrinkle, held, arrived):
    rows = held.shape[2] // 2
    copies = {}
    for sub in range(2):
        for half in range(2):
            at = pl.ds(half * rows, rows)
            copies[sub, half] = [
                pltpu.make_async_copy(
                    source.at[0, sub, at], held.at[sub, which, at], arrived.at[sub, half, which]
                )
                for which, source in enumerate((taut, wrinkle))
            ]
    return copies


def start_loads(copies):
    for pair in copies.values():
        for copy in pair:
            copy.start()


def product(copies, flags, held, vectors, result, outgoing, rows):
    east, west, south, north = outgoing
    for (sub, half), pair in copies.items():
        for copy in pair:
            copy.wait()
        own = vectors[sub]
        at = slice(2 * rows * half, 2 * rows * (half + 1))
        flag = flags[sub].astype(F32)
        value = dot(held[sub, 0, at], own) + flag * dot(held[sub, 1, at], own)
        near, far = value[:rows], value[rows:]
        result[sub, 2 * half] = near
        result[sub, 2 * half + 1] = far
        if half == 0:
            if sub == 1:
                east[0, :rows] = near.astype(BF16)
            south[sub, :rows] = far.astype(BF16)
        else:
            if sub == 0:
                west[0, :rows] = near.astype(BF16)
            north[sub, :rows] = far.astype(BF16)


def product_call(
    body, flags, taut, wrinkle, others, specs, rows, extra_rows, more_out=(), more_scratch=(),
    limit=PRODUCT_VMEM,
):
    order = 4 * rows
    sent = rows + extra_rows
    outs = [
        jax.ShapeDtypeStruct((2, 4, rows, LANES), F32),
        jax.ShapeDtypeStruct((1, sent, LANES), BF16),
        jax.ShapeDtypeStruct((1, sent, LANES), BF16),
        jax.ShapeDtypeStruct((2, sent, LANES), BF16),
        jax.ShapeDtypeStruct((2, sent, LANES), BF16),
        *more_out,
    ]
    return pl.pallas_call(
        body,
        out_shape=outs,
        in_specs=[SMEM, HBM, HBM, *specs],
        out_specs=[VMEM] * len(outs),
        scratch_shapes=[
            pltpu.VMEM((2, order, LANES), BF16),
            pltpu.VMEM((2, 2, order, order), BF16),
            pltpu.SemaphoreType.DMA((2, 2, 2)),
            *more_scratch,
        ],
        compiler_params=pltpu.CompilerParams(vmem_limit_bytes=limit),
    )(flags, taut, wrinkle, *others)


def live_length(spots, lengths, sub, kind, last):
    exists = 2 * spots[1] + sub < last[0] if kind == EAST else spots[0] < last[1]
    return jnp.where(exists, lengths[sub, kind], 0)


def pack_body(last, spots, lengths, loads, east, south):
    rows = loads.shape[2]
    for target, slot, sub, kind in (
        (east, 0, 1, EAST), (south, 0, 0, SOUTH), (south, 1, 1, SOUTH)
    ):
        length = live_length(spots, lengths, sub, kind, last)
        live = lax.broadcasted_iota(jnp.int32, (rows, LANES), 0) < length
        target[slot, :rows] = jnp.where(live, 0.5 * loads[sub, kind], 0.0).astype(BF16)
        upper = lax.broadcasted_iota(jnp.int32, (LEN_ROWS, LANES), 0) < LEN_ROWS // 2
        digits = jnp.where(upper, length >> 4, length & 15)
        target[slot, rows:] = digits.astype(F32).astype(BF16)


def first_body(last, flags, taut, wrinkle, spots, lengths, loads, from_left, from_up, pieces,
               result, east, west, south, north, lens, start, vectors, held, arrived):
    rows = loads.shape[2]
    copies = loads_of(taut, wrinkle, held, arrived)
    start_loads(copies)

    def limit(rows_of):
        return rows_of[0:8].astype(F32) * 16.0 + rows_of[8:16].astype(F32)

    for sub in range(2):
        for kind in (EAST, SOUTH):
            length = live_length(spots, lengths, sub, kind, last)
            live = lax.broadcasted_iota(jnp.int32, (rows, LANES), 0) < length
            start[sub, kind] = jnp.where(live, 0.5 * loads[sub, kind], 0.0)
            lens[sub, kind] = jnp.broadcast_to(length, (8, LANES)).astype(F32)
        start[sub, NORTH] = -from_up[sub, :rows].astype(F32)
        lens[sub, NORTH] = limit(from_up[sub, rows:])
        south[sub, rows:] = pieces[sub, SOUTH]
        north[sub, rows:] = pieces[sub, NORTH]
    start[0, WEST] = -from_left[0, :rows].astype(F32)
    start[1, WEST] = -start[0, EAST]
    lens[0, WEST] = limit(from_left[0, rows:])
    lens[1, WEST] = lens[0, EAST]
    east[0, rows:] = pieces[1, EAST]
    west[0, rows:] = pieces[0, WEST]
    for sub in range(2):
        for kind in range(4):
            vectors[sub, kind * rows : (kind + 1) * rows] = start[sub, kind].astype(BF16)
    product(copies, flags, held, vectors, result, (east, west, south, north), rows)


def partner(result, incoming, sub, kind, rows):
    east, west, south, north = incoming
    if kind == EAST:
        return result[1, WEST] if sub == 0 else east[0, :rows].astype(F32)
    if kind == WEST:
        return result[0, EAST] if sub == 1 else west[0, :rows].astype(F32)
    if kind == SOUTH:
        return south[sub, :rows].astype(F32)
    return north[sub, :rows].astype(F32)


def preconditioned_part(result, incoming, lens, sub, kind, rows):
    gap = result[sub, kind] - partner(result, incoming, sub, kind, rows)
    return jnp.where(below(lens[sub, kind, 0:1], rows), 0.5 * gap, 0.0)


def fill_multipliers(number, result, incoming, lens, earlier, kept, vectors):
    rows = result.shape[2]
    for sub in range(2):
        for kind in range(4):
            part = preconditioned_part(result, incoming, lens, sub, kind, rows)
            if number == 0:
                total = step_sizes[0] * part
                if kept is not None:
                    kept[sub, kind] = part
            else:
                before = earlier[sub, kind]
                total = step_sizes[0] * before + step_sizes[1] * (part + momenta[1] * before)
                if kept is not None and kind < 2:
                    kept[sub, kind] = total
            vectors[sub, kind * rows : (kind + 1) * rows] = total.astype(BF16)


def coarse_terms(coupling, vectors, terms, stacked):
    for sub in range(2):
        stacked[sub * CORNERS : (sub + 1) * CORNERS] = dot(coupling[0, sub], vectors[sub])
    terms[...] = stacked[...].astype(BF16)


def first_terms_body(result, east, west, south, north, lens, coupling, pieces,
                     terms, vectors, kept, paired, stacked):
    rows = result.shape[2]
    fill_multipliers(0, result, (east, west, south, north), lens, None, kept, vectors)
    coarse_terms(coupling, vectors, terms, stacked)
    other = {
        (0, EAST): pieces[1, WEST],
        (1, WEST): pieces[0, EAST],
        (0, NORTH): north[0, rows:],
        (1, NORTH): north[1, rows:],
        (0, SOUTH): south[0, rows:],
        (1, SOUTH): south[1, rows:],
        (0, WEST): west[0, rows:],
        (1, EAST): east[0, rows:],
    }
    for (sub, kind), piece in other.items():
        for segment in range(pieces.shape[2] // SLOT):
            at = slice(segment * SLOT, (segment + 1) * SLOT)
            low = 2 * segment * SLOT
            paired[sub, kind, low : low + SLOT] = pieces[sub, kind, at]
            paired[sub, kind, low + SLOT : low + 2 * SLOT] = piece[at]


def second_terms_body(result, east, west, south, north, lens, coupling, earlier,
                      terms, vectors, kept, stacked):
    fill_multipliers(1, result, (east, west, south, north), lens, earlier, kept, vectors)
    coarse_terms(coupling, vectors, terms, stacked)


def terms_call(number, result, incoming, lens, coupling, extra):
    rows = result.shape[2]
    outs = [
        jax.ShapeDtypeStruct((2 * CORNERS, LANES), BF16),
        jax.ShapeDtypeStruct((2, 4 * rows, LANES), BF16),
        jax.ShapeDtypeStruct((2, 4 - 2 * number, rows, LANES), F32),
    ]
    if number == 0:
        outs.append(jax.ShapeDtypeStruct((2, 4, 2 * extra.shape[2], LANES), BF16))
    return pl.pallas_call(
        second_terms_body if number else first_terms_body,
        out_shape=outs,
        in_specs=[VMEM] * 8,
        out_specs=[VMEM] * len(outs),
        scratch_shapes=[pltpu.VMEM((2 * CORNERS, LANES), F32)],
        compiler_params=pltpu.CompilerParams(vmem_limit_bytes=SMALL_VMEM),
    )(result, *incoming, lens, coupling, extra)


def dual_body(flags, taut, wrinkle, source, result, east, west, south, north,
              vectors, held, arrived, loaded):
    rows = result.shape[2]
    own = pltpu.make_async_copy(source, vectors, loaded)
    own.start()
    copies = loads_of(taut, wrinkle, held, arrived)
    start_loads(copies)
    own.wait()
    product(copies, flags, held, vectors, result, (east, west, south, north), rows)


def correction_body(terms, select, paired, start, lens, out):
    rows = start.shape[2]
    solved = dot(select[...], terms[...]).astype(BF16)
    group = [solved[SLOT * k : SLOT * (k + 1)] for k in range(8)]
    other = {
        (0, EAST): group[1],
        (1, WEST): group[0],
        (0, NORTH): group[2],
        (1, NORTH): group[3],
        (0, SOUTH): group[4],
        (1, SOUTH): group[5],
        (0, WEST): group[6],
        (1, EAST): group[7],
    }
    for (sub, kind), values in other.items():
        stacked = jnp.concatenate([group[sub], -values], axis=0)
        for segment in range(paired.shape[2] // (2 * SLOT)):
            low = segment * LANES
            high = min(rows, low + LANES)
            both = paired[sub, kind, 2 * segment * SLOT : 2 * (segment + 1) * SLOT]
            shift = dot(both, stacked, ((0,), (0,)))[: high - low]
            spot = lax.broadcasted_iota(jnp.int32, (high - low, LANES), 0) + low
            live = spot.astype(F32) < lens[sub, kind, 0:1]
            out[sub, kind, low:high] = start[sub, kind, low:high] - jnp.where(
                live, 0.5 * shift, 0.0
            )


def correction_call(*operands):
    rows = operands[3].shape[2]
    return pl.pallas_call(
        correction_body,
        out_shape=jax.ShapeDtypeStruct((2, 4, rows, LANES), F32),
        in_specs=[VMEM] * len(operands),
        out_specs=VMEM,
        compiler_params=pltpu.CompilerParams(vmem_limit_bytes=SMALL_VMEM),
    )(*operands)


def residual_body(flags, taut, wrinkle, earlier, from_east, from_west, from_south, from_north,
                  lens, base, result, east, west, south, north, vectors, held, arrived):
    rows = earlier.shape[2]
    incoming = (from_east, from_west, from_south, from_north)
    copies = loads_of(taut, wrinkle, held, arrived)
    start_loads(copies)
    for sub in range(2):
        for kind in range(4):
            gap = preconditioned_part(earlier, incoming, lens, sub, kind, rows)
            vectors[sub, kind * rows : (kind + 1) * rows] = (base[sub, kind] - gap).astype(BF16)
    product(copies, flags, held, vectors, result, (east, west, south, north), rows)


def last_body(result, east, south, lens, out):
    rows = result.shape[2]
    for sub in range(2):
        for kind in range(2):
            out[sub, kind] = preconditioned_part(
                result, (east, None, south, None), lens, sub, kind, rows
            )


def coarse_rows(coarse_inverse, corner_map):
    row_count, col_count = coarse_inverse.shape
    rows_of = lax.axis_size("sx")
    cols_of = lax.axis_size("sy")
    per = 2 * CORNERS
    row_index = lax.axis_index("sx")
    row_maps = copies_of_all(corner_map.reshape(1, per), "sy").reshape(cols_of * per)
    codes = jnp.concatenate([row_maps // 32, row_maps % 32]).astype(BF16)
    code_rows = codes.shape[0] // LANES
    tile = jnp.pad(coarse_inverse, ((0, 0), (0, LANES - col_count)))
    message = jnp.concatenate([tile, codes.reshape(code_rows, LANES)], axis=0)
    message = jnp.pad(message, ((0, 64 - message.shape[0]), (0, 0)))
    arrived = copies_of_all(message, "sx")
    columns = arrived[:, :row_count].reshape(rows_of * row_count, LANES)
    codes = arrived[:, row_count : row_count + code_rows].astype(jnp.int32)
    codes = codes.reshape(rows_of, 2, cols_of, per)
    maps = codes[:, 0] * 32 + codes[:, 1]
    at = lambda by: lax.dynamic_index_in_dim(maps, (row_index + by) % rows_of, 0, False)
    here, up, down = at(0), at(-1 + rows_of), at(1)
    groups = [
        here[:, :CORNERS],
        here[:, CORNERS:],
        up[:, :CORNERS],
        up[:, CORNERS:],
        down[:, :CORNERS],
        down[:, CORNERS:],
        jnp.roll(here, 1, axis=0)[:, CORNERS:],
        jnp.roll(here, -1, axis=0)[:, :CORNERS],
    ]
    wanted = jnp.pad(
        jnp.stack(groups, axis=1), ((0, 0), (0, 0), (0, SLOT - CORNERS)), constant_values=-1
    ).reshape(-1, 1)
    coarse_order = rows_of * row_count
    pick = (wanted == jnp.arange(coarse_order)[None]).astype(BF16)
    chosen = dot(pick, columns).astype(BF16).reshape(cols_of, -1, LANES)
    chosen = lax.all_to_all(chosen, "sy", 0, 0, tiled=True)
    flat = maps.reshape(-1)
    spot = (flat // col_count) * LANES + flat % col_count
    place = (jnp.arange(cols_of * LANES)[:, None] == spot[None]).astype(BF16)
    chosen = jnp.moveaxis(chosen, 0, 1).reshape(chosen.shape[1], -1)
    return dot(chosen, place).astype(BF16)


def steps(
    adjoint_loads,
    dual_taut,
    dual_wrinkle,
    dirichlet_taut,
    dirichlet_wrinkle,
    coupling,
    coarse_inverse,
    wrinkled,
    edge_lengths,
    corner_map,
):
    rows = adjoint_loads.shape[3]
    loads = adjoint_loads[0]
    flags = wrinkled[0]
    lengths = edge_lengths[0]
    spots = jnp.stack([lax.axis_index("sx"), lax.axis_index("sy")]).astype(jnp.int32)
    last = (2 * lax.axis_size("sy") - 1, lax.axis_size("sx") - 1)
    east, south = pl.pallas_call(
        functools.partial(pack_body, last),
        out_shape=[
            jax.ShapeDtypeStruct((1, rows + LEN_ROWS, LANES), BF16),
            jax.ShapeDtypeStruct((2, rows + LEN_ROWS, LANES), BF16),
        ],
        in_specs=[SMEM, SMEM, VMEM],
        out_specs=[VMEM] * 2,
        compiler_params=pltpu.CompilerParams(vmem_limit_bytes=SMALL_VMEM),
    )(spots, lengths, loads)
    _, from_left, _, from_up = exchanged((east, None, south, None))

    segments = -(-rows // LANES)
    pieces = coupling[0].reshape(2, CORNERS, 4, rows)
    pieces = jnp.pad(
        pieces, ((0, 0), (0, SLOT - CORNERS), (0, 0), (0, segments * LANES - rows))
    )
    pieces = pieces.reshape(2, SLOT, 4, segments, LANES)
    pieces = jnp.transpose(pieces, (0, 2, 3, 1, 4)).reshape(2, 4, segments * SLOT, LANES)
    select = coarse_rows(coarse_inverse, corner_map)

    result, *outgoing, lens, start = product_call(
        functools.partial(first_body, last), flags, dirichlet_taut, dirichlet_wrinkle,
        (spots, lengths, loads, from_left, from_up, pieces), [SMEM] * 2 + [VMEM] * 4,
        rows, segments * SLOT,
        (
            jax.ShapeDtypeStruct((2, 4, 8, LANES), F32),
            jax.ShapeDtypeStruct((2, 4, rows, LANES), F32),
        ),
    )
    for number in range(2):
        incoming = exchanged(outgoing)
        if number == 0:
            terms, vectors, kept, paired = terms_call(
                0, result, incoming, lens, coupling, pieces
            )
        else:
            terms, vectors, kept = terms_call(1, result, incoming, lens, coupling, kept)
        everyone = copies_of_all(terms, ("sx", "sy")).reshape(-1, LANES)
        result, *outgoing = product_call(
            dual_body, flags, dual_taut, dual_wrinkle, (vectors,), [HBM],
            rows, 0, (), [pltpu.SemaphoreType.DMA],
        )
        incoming = exchanged(outgoing)
        base = correction_call(everyone, select, paired, start, lens)
        result, *outgoing = product_call(
            residual_body, flags, dirichlet_taut, dirichlet_wrinkle,
            (result, *incoming, lens, base), [VMEM] * 7, rows, 0,
        )
    _, west, _, north = outgoing
    from_east, _, from_south, _ = exchanged((None, west, None, north))
    preconditioned = pl.pallas_call(
        last_body,
        out_shape=jax.ShapeDtypeStruct((2, 2, rows, LANES), F32),
        in_specs=[VMEM] * 4,
        out_specs=VMEM,
        compiler_params=pltpu.CompilerParams(vmem_limit_bytes=SMALL_VMEM),
    )(result, from_east, from_south, lens)
    return kept[None], preconditioned[None]


def solution(mesh):
    placed = (
        P("sx", "sy", None, None, None),
        P("sx", "sy", None, None),
        P("sx", "sy", None, None),
        P("sx", "sy", None, None),
        P("sx", "sy", None, None),
        P("sx", "sy", None, None),
        P("sx", "sy"),
        P("sx", "sy"),
        P("sx", "sy", None),
        P("sx", "sy", None),
    )
    return jax.shard_map(
        steps,
        mesh=mesh,
        in_specs=placed,
        out_specs=(P("sx", "sy", None, None, None), P("sx", "sy", None, None, None)),
        check_vma=False,
    )
```

profile of v0, /device:TPU:1, one launch (start us, length us, event | category | flops | bytes accessed | tf_op | source)
XLA Modules:
  0.0 156.4 jit_solution(5304386395264528855)
XLA Ops:
  1.4 14.6 %all_to_all.25 = s32[8,1,24]{2,1,0:T(1,128)S(1)} all-to-all(s32[8,1,24]{2,1,0:T(1,128)S(1)} %broadcast_in_dim.16), channel_id=1, replica_groups=mesh['sx'=16,'sy'=8] {'sy'}, dimensions={0} | all-to-all | bytes 1536 | tf_op jit(solution)/shard_map/all_to_all | solution.py:33
  18.9 6.7 %all-to-all-start.2 = ((bf16[16,64,128]{2,1,0:T(8,128)(2,1)}), bf16[16,64,128]{2,1,0:T(8,128)(2,1)S(1)}, u32[]{:S(2)}, u32[]{:S(2)}) async-start(bf16[16,64,128]{2,1,0:T(8,128)(2,1)} %broadcast_in_dim.17), calls=%async_computation.2 | async-start | bytes 524288 | tf_op jit(solution)/shard_map/all_to_all | solution.py:33
  30.4 2.5 %all-to-all-done.2 = bf16[16,64,128]{2,1,0:T(8,128)(2,1)S(1)} async-done(((bf16[16,64,128]{2,1,0:T(8,128)(2,1)}), bf16[16,64,128]{2,1,0:T(8,128)(2,1)S(1)}, u32[]{:S(2)}, u32[]{:S(2)}) %all-to-all-start.2) | async-done | bytes 262176 | tf_op jit(solution)/shard_map/all_to_all | solution.py:33
  35.2 4.2 %all-to-all-start.3 = ((bf16[8,128,128]{1,2,0:T(8,128)(2,1)}), bf16[8,128,128]{1,2,0:T(8,128)(2,1)}, u32[]{:S(2)}, u32[]{:S(2)}) async-start(bf16[8,128,128]{1,2,0:T(8,128)(2,1)} %copy.18), calls=%async_computation.3 | async-start | bytes 524288 | tf_op jit(solution)/shard_map/all_to_all | solution.py:375
  39.7 5.7 %shard_map.114 = (f32[2,4,288,128]{3,2,1,0:T(8,128)S(1)}, bf16[1,336,128]{2,1,0:T(8,128)(2,1)S(1)}, bf16[1,336,128]{2,1,0:T(8,128)(2,1)S(1)}, bf16[2,336,128]{2,...) custom-call(s32[2]{0:T(128)S(1)} %bitcast.70, ...), custom_call_target="tpu_custom_call" | custom-call | tf_op jit(solution)/shard_map/pallas_call | solution.py:117
  47.2 5.2 %collective-permute-start.2 = (bf16[1,336,128]{2,1,0:T(8,128)(2,1)S(1)}, bf16[1,336,128]{2,1,0:T(8,128)(2,1)S(1)}, u32[]{:S(2)}, u32[]{:S(2)}) collective-permute-start(bf16[1,336,128]{2,1,0:T(8,128)(2,1)S(1)} %get-tuple-element.39), channel_id=1, source_target_pairs={{0,7},{1,0},{2,1},{3,2},{4,3},{5,4},{6,5},{7,6},{8,15},{9,8},{10,9... | collective-permute-start | bytes 258056 | tf_op jit(solution)/shard_map/ppermute | solution.py:28
  52.5 4.3 %collective-permute-done.2.east = bf16[1,336,128]{2,1,0:T(8,128)(2,1)S(1)} collective-permute-done((bf16[1,336,128]{2,1,0:T(8,128)(2,1)S(1)}, bf16[1,336,128]{2,1,0:T(8,128)(2,1)S(1)}, u32[]{:S(2)}, u32[]{:S(2)}) %collective-permute-start.2) | collective-permute-done | bytes 86048 | tf_op jit(solution)/shard_map/ppermute | solution.py:28
  56.8 3.9 %collective-permute-done.3.west = bf16[1,336,128]{2,1,0:T(8,128)(2,1)S(1)} collective-permute-done((bf16[1,336,128]{2,1,0:T(8,128)(2,1)S(1)}, bf16[1,336,128]{2,1,0:T(8,128)(2,1)S(1)}, u32[]{:S(2)}, u32[]{:S(2)}) %collective-permute-start.3) | collective-permute-done | bytes 86048 | tf_op jit(solution)/shard_map/ppermute | solution.py:28
  63.3 4.2 %all-to-all-start = ((bf16[128,24,128]{2,1,0:T(8,128)(2,1)}), bf16[128,24,128]{2,1,0:T(8,128)(2,1)S(1)}, u32[]{:S(2)}, u32[]{:S(2)}) async-start(bf16[128,24,128]{2,1,0:T(8,128)(2,1)} %broadcast_in_dim.14), calls=%async_computation | async-start | bytes 1572864 | tf_op jit(solution)/shard_map/all_to_all | solution.py:33
  67.8 6.5 %shard_map.116 = (f32[2,4,288,128]{3,2,1,0:T(8,128)S(1)}, bf16[1,288,128]{2,1,0:T(8,128)(2,1)}, bf16[1,288,128]{2,1,0:T(8,128)(2,1)}, bf16[2,288,128]{2,1,0:T(8,128)(2,1)}, bf16[2,288,128]{2,1,0:T(8,128)(2,1)}) custom-call(s32[2]{0:T(128)S(1)} %bitcast.71, bf16[1,2,1152,1152]{3,2,1,0:T(8,128)(2,1)} %taut.8, bf16[1,2,1152,1152]{3,2,1,0:T(8,128)(2,1)} %wrinkle.8, ...), custom_call_target="tpu_custom_call" | custom-call | tf_op jit(solution)/shard_map/pallas_call | solution.py:117
  75.4 5.8 %collective-permute-start.6 = (bf16[1,288,128]{2,1,0:T(8,128)(2,1)}, bf16[1,288,128]{2,1,0:T(8,128)(2,1)S(1)}, u32[]{:S(2)}, u32[]{:S(2)}) collective-permute-start(bf16[1,288,128]{2,1,0:T(8,128)(2,1)} %get-tuple-element.46), channel_id=1, source_target_pairs={{0,7},{1,0},{2,1},{3,2},{4,3},{5,4},{6,5},{7,6},{8,15},{9,8},{10,9... | collective-permute-start | bytes 221192 | tf_op jit(solution)/shard_map/ppermute | solution.py:28
  83.0 3.5 %fusion.3.select = bf16[128,3072]{1,0:T(8,128)(2,1)S(1)} fusion(bf16[128,1024]{0,1:T(8,128)(2,1)} %bitcast.28, s32[3072]{0:T(1024)S(1)} %fusion.9), kind=kOutput, calls=%fused_computation.5 | convolution fusion | flops 808845312 | bytes 1060864 | tf_op jit(solution)/shard_map/dot_general | solution.py:48
  89.3 5.7 %shard_map.118 = (f32[2,4,288,128]{3,2,1,0:T(8,128)S(1)}, bf16[1,288,128]{2,1,0:T(8,128)(2,1)S(1)}, bf16[1,288,128]{2,1,0:T(8,128)(2,1)S(1)}, bf16[2,288,128]{2,1,0:T(8,128)(2,1)S(1)}, bf16[2,288,128]{2,1,0:T(8,128)(2,1)S(1)}) custom-call(s32[2]{0:T(128)S(1)} %bitcast.72, bf16[1,2,1152,1152]{3,2,1,0:T(8,128)(2,1)} %taut.9, ...), custom_call_target="tpu_custom_call" | custom-call | tf_op jit(solution)/shard_map/pallas_call | solution.py:117
  95.0 2.8 %collective-permute-start.12 = (bf16[2,288,128]{2,1,0:T(8,128)(2,1)S(1)}, bf16[2,288,128]{2,1,0:T(8,128)(2,1)S(1)}, u32[]{:S(2)}, u32[]{:S(2)}) collective-permute-start(bf16[2,288,128]{2,1,0:T(8,128)(2,1)S(1)} %get-tuple-element.56), channel_id=1, source_target_pairs={{0,120},{8,0},{16,8},{24,16},{32,24},{40,32},{48,40},{56,48},{64,5... | collective-permute-start | bytes 442376 | tf_op jit(solution)/shard_map/ppermute | solution.py:28
  97.8 4.8 %collective-permute-start.10 = (bf16[1,288,128]{2,1,0:T(8,128)(2,1)S(1)}, bf16[1,288,128]{2,1,0:T(8,128)(2,1)S(1)}, u32[]{:S(2)}, u32[]{:S(2)}) collective-permute-start(bf16[1,288,128]{2,1,0:T(8,128)(2,1)S(1)} %get-tuple-element.54), channel_id=1, source_target_pairs={{0,7},{1,0},{2,1},{3,2},{4,3},{5,4},{6,5},{7,6},{8,15},{9,8},{10,9... | collective-permute-start | bytes 221192 | tf_op jit(solution)/shard_map/ppermute | solution.py:28
  104.0 5.4 %collective-permute-done.11.west = bf16[1,288,128]{2,1,0:T(8,128)(2,1)S(1)} collective-permute-done((bf16[1,288,128]{2,1,0:T(8,128)(2,1)S(1)}, bf16[1,288,128]{2,1,0:T(8,128)(2,1)S(1)}, u32[]{:S(2)}, u32[]{:S(2)}) %collective-permute-start.11) | collective-permute-done | bytes 73760 | tf_op jit(solution)/shard_map/ppermute | solution.py:28
  111.9 6.6 %all-to-all-start.4 = ((bf16[128,24,128]{2,1,0:T(8,128)(2,1)}), bf16[128,24,128]{2,1,0:T(8,128)(2,1)S(1)}, u32[]{:S(2)}, u32[]{:S(2)}) async-start(bf16[128,24,128]{2,1,0:T(8,128)(2,1)} %broadcast_in_dim.19), calls=%async_computation.4 | async-start | bytes 1572864 | tf_op jit(solution)/shard_map/all_to_all | solution.py:33
  119.6 6.5 %shard_map.120 = (f32[2,4,288,128]{3,2,1,0:T(8,128)S(1)}, bf16[1,288,128]{2,1,0:T(8,128)(2,1)S(1)}, bf16[1,288,128]{2,1,0:T(8,128)(2,1)}, bf16[2,288,128]{2,1,0:T(8,128)(2,1)}, bf16[2,288,128]{2,1,0:T(8,128)(2,1)}) custom-call(s32[2]{0:T(128)S(1)} %bitcast.73, bf16[1,2,1152,1152]{3,2,1,0:T(8,128)(2,1)} %taut.8, bf16[1,2,1152,1152]{3,2,1,0:T(8,128)(2,1)} %wrinkle.8, ...), custom_call_target="tpu_custom_call" | custom-call | tf_op jit(solution)/shard_map/pallas_call | solution.py:117
  127.2 1.4 collective-permute-start.16
  128.9 5.8 %collective-permute-start.14 = (bf16[1,288,128]{2,1,0:T(8,128)(2,1)}, bf16[1,288,128]{2,1,0:T(8,128)(2,1)S(1)}, u32[]{:S(2)}, u32[]{:S(2)}) collective-permute-start(bf16[1,288,128]{2,1,0:T(8,128)(2,1)} %get-tuple-element.62), channel_id=1, source_target_pairs={{0,7},{1,0},{2,1},{3,2},{4,3},{5,4},{6,5},{7,6},{8,15},{9,8},{10,9... | collective-permute-start | bytes 221192 | tf_op jit(solution)/shard_map/ppermute | solution.py:28
  136.5 5.1 %collective-permute-done.15.from_west = bf16[1,288,128]{2,1,0:T(8,128)(2,1)S(1)} collective-permute-done((bf16[1,288,128]{2,1,0:T(8,128)(2,1)S(1)}, bf16[1,288,128]{2,1,0:T(8,128)(2,1)S(1)}, u32[]{:S(2)}, u32[]{:S(2)}) %collective-permute-start.15) | collective-permute-done | bytes 73760 | tf_op jit(solution)/shard_map/ppermute | solution.py:28
  141.6 5.7 %shard_map.122 = (f32[2,4,288,128]{3,2,1,0:T(8,128)S(1)}, bf16[1,288,128]{2,1,0:T(8,128)(2,1)}, bf16[1,288,128]{2,1,0:T(8,128)(2,1)S(1)}, bf16[2,288,128]{2,1,0:T(8,128)(2,1)}, bf16[2,288,128]{2,1,0:T(8,128)(2,1)S(1)}) custom-call(s32[2]{0:T(128)S(1)} %bitcast.74, bf16[1,2,1152,1152]{3,2,1,0:T(8,128)(2,1)} %taut.9, bf16[1,2,1152,1152]{3,2,1,0:T(8,128)(2,1)} %wrinkle.9, ...), custom_call_target="tpu_custom_call" | custom-call | tf_op jit(solution)/shard_map/pallas_call | solution.py:117
  147.3 3.4 %collective-permute-start.19 = (bf16[2,288,128]{2,1,0:T(8,128)(2,1)S(1)}, bf16[2,288,128]{2,1,0:T(8,128)(2,1)S(1)}, u32[]{:S(2)}, u32[]{:S(2)}) collective-permute-start(bf16[2,288,128]{2,1,0:T(8,128)(2,1)S(1)} %get-tuple-element.69), channel_id=1, source_target_pairs={{0,120},{8,0},{16,8},{24,16},{32,24},{40,32},{48,40},{56,48},{64,5... | collective-permute-start | bytes 442376 | tf_op jit(solution)/shard_map/ppermute | solution.py:28
  150.7 4.8 %collective-permute-done.18.east = bf16[1,288,128]{2,1,0:T(8,128)(2,1)S(1)} collective-permute-done((bf16[1,288,128]{2,1,0:T(8,128)(2,1)S(1)}, bf16[1,288,128]{2,1,0:T(8,128)(2,1)S(1)}, u32[]{:S(2)}, u32[]{:S(2)}) %collective-permute-start.18) | collective-permute-done | bytes 73760 | tf_op jit(solution)/shard_map/ppermute | solution.py:28
  (110 shorter events, 30.1 us)
Async XLA Ops:
  18.9 13.9 %all-to-all-start.2 = ((bf16[16,64,128]{2,1,0:T(8,128)(2,1)}), bf16[16,64,128]{2,1,0:T(8,128)(2,1)S(1)}, u32[]{:S(2)}, u32[]{:S(2)}) async-start(bf16[16,64,128]{2,1,0:T(8,128)(2,1)} %broadcast_in_dim.17), calls=%async_computation.2 | async-start | bytes 524288 | tf_op jit(solution)/shard_map/all_to_all | solution.py:33
  28.1 11.5 %collective-permute-start = (bf16[1,304,128]{2,1,0:T(8,128)(2,1)S(1)}, bf16[1,304,128]{2,1,0:T(8,128)(2,1)S(1)}, u32[]{:S(2)}, u32[]{:S(2)}) collective-permute-start(bf16[1,304,128]{2,1,0:T(8,128)(2,1)S(1)} %get-tuple-element.36), channel_id=1, source_target_pairs={{0,1},{1,2},{2,3},{3,4},{4,5},{5,6},{6,7},{7,0},{8,9},{9,10},{10,1... | collective-permute-start | bytes 233480 | tf_op jit(solution)/shard_map/ppermute | solution.py:28
  29.1 10.6 %collective-permute-start.1 = (bf16[2,304,128]{2,1,0:T(8,128)(2,1)S(1)}, bf16[2,304,128]{2,1,0:T(8,128)(2,1)S(1)}, u32[]{:S(2)}, u32[]{:S(2)}) collective-permute-start(bf16[2,304,128]{2,1,0:T(8,128)(2,1)S(1)} %get-tuple-element.37), channel_id=1, source_target_pairs={{0,8},{8,16},{16,24},{24,32},{32,40},{40,48},{48,56},{56,64},{64,7... | collective-permute-start | bytes 466952 | tf_op jit(solution)/shard_map/ppermute | solution.py:28
  35.2 27.2 %all-to-all-start.3 = ((bf16[8,128,128]{1,2,0:T(8,128)(2,1)}), bf16[8,128,128]{1,2,0:T(8,128)(2,1)}, u32[]{:S(2)}, u32[]{:S(2)}) async-start(bf16[8,128,128]{1,2,0:T(8,128)(2,1)} %copy.18), calls=%async_computation.3 | async-start | bytes 524288 | tf_op jit(solution)/shard_map/all_to_all | solution.py:375
  45.4 15.3 %collective-permute-start.4 = (bf16[2,336,128]{2,1,0:T(8,128)(2,1)S(1)}, bf16[2,336,128]{2,1,0:T(8,128)(2,1)S(1)}, u32[]{:S(2)}, u32[]{:S(2)}) collective-permute-start(bf16[2,336,128]{2,1,0:T(8,128)(2,1)S(1)} %get-tuple-element.41), channel_id=1, source_target_pairs={{0,120},{8,0},{16,8},{24,16},{32,24},{40,32},{48,40},{56,48},{64,5... | collective-permute-start | bytes 516104 | tf_op jit(solution)/shard_map/ppermute | solution.py:28
  46.5 14.2 %collective-permute-start.5 = (bf16[2,336,128]{2,1,0:T(8,128)(2,1)S(1)}, bf16[2,336,128]{2,1,0:T(8,128)(2,1)S(1)}, u32[]{:S(2)}, u32[]{:S(2)}) collective-permute-start(bf16[2,336,128]{2,1,0:T(8,128)(2,1)S(1)} %get-tuple-element.42), channel_id=1, source_target_pairs={{0,8},{8,16},{16,24},{24,32},{32,40},{40,48},{48,56},{56,64},{64,7... | collective-permute-start | bytes 516104 | tf_op jit(solution)/shard_map/ppermute | solution.py:28
  47.2 9.6 %collective-permute-start.2 = (bf16[1,336,128]{2,1,0:T(8,128)(2,1)S(1)}, bf16[1,336,128]{2,1,0:T(8,128)(2,1)S(1)}, u32[]{:S(2)}, u32[]{:S(2)}) collective-permute-start(bf16[1,336,128]{2,1,0:T(8,128)(2,1)S(1)} %get-tuple-element.39), channel_id=1, source_target_pairs={{0,7},{1,0},{2,1},{3,2},{4,3},{5,4},{6,5},{7,6},{8,15},{9,8},{10,9... | collective-permute-start | bytes 258056 | tf_op jit(solution)/shard_map/ppermute | solution.py:28
  52.5 8.3 %collective-permute-start.3 = (bf16[1,336,128]{2,1,0:T(8,128)(2,1)S(1)}, bf16[1,336,128]{2,1,0:T(8,128)(2,1)S(1)}, u32[]{:S(2)}, u32[]{:S(2)}) collective-permute-start(bf16[1,336,128]{2,1,0:T(8,128)(2,1)S(1)} %get-tuple-element.40), channel_id=1, source_target_pairs={{0,1},{1,2},{2,3},{3,4},{4,5},{5,6},{6,7},{7,0},{8,9},{9,10},{10,1... | collective-permute-start | bytes 258056 | tf_op jit(solution)/shard_map/ppermute | solution.py:28
  63.3 23.2 %all-to-all-start = ((bf16[128,24,128]{2,1,0:T(8,128)(2,1)}), bf16[128,24,128]{2,1,0:T(8,128)(2,1)S(1)}, u32[]{:S(2)}, u32[]{:S(2)}) async-start(bf16[128,24,128]{2,1,0:T(8,128)(2,1)} %broadcast_in_dim.14), calls=%async_computation | async-start | bytes 1572864 | tf_op jit(solution)/shard_map/all_to_all | solution.py:33
  75.4 11.8 %collective-permute-start.6 = (bf16[1,288,128]{2,1,0:T(8,128)(2,1)}, bf16[1,288,128]{2,1,0:T(8,128)(2,1)S(1)}, u32[]{:S(2)}, u32[]{:S(2)}) collective-permute-start(bf16[1,288,128]{2,1,0:T(8,128)(2,1)} %get-tuple-element.46), channel_id=1, source_target_pairs={{0,7},{1,0},{2,1},{3,2},{4,3},{5,4},{6,5},{7,6},{8,15},{9,8},{10,9... | collective-permute-start | bytes 221192 | tf_op jit(solution)/shard_map/ppermute | solution.py:28
  81.2 7.0 %collective-permute-start.7 = (bf16[1,288,128]{2,1,0:T(8,128)(2,1)}, bf16[1,288,128]{2,1,0:T(8,128)(2,1)S(1)}, u32[]{:S(2)}, u32[]{:S(2)}) collective-permute-start(bf16[1,288,128]{2,1,0:T(8,128)(2,1)} %get-tuple-element.47), channel_id=1, source_target_pairs={{0,1},{1,2},{2,3},{3,4},{4,5},{5,6},{6,7},{7,0},{8,9},{9,10},{10,1... | collective-permute-start | bytes 221192 | tf_op jit(solution)/shard_map/ppermute | solution.py:28
  81.2 8.1 %collective-permute-start.8 = (bf16[2,288,128]{2,1,0:T(8,128)(2,1)}, bf16[2,288,128]{2,1,0:T(8,128)(2,1)S(1)}, u32[]{:S(2)}, u32[]{:S(2)}) collective-permute-start(bf16[2,288,128]{2,1,0:T(8,128)(2,1)} %get-tuple-element.48), channel_id=1, source_target_pairs={{0,120},{8,0},{16,8},{24,16},{32,24},{40,32},{48,40},{56,48},{64,5... | collective-permute-start | bytes 442376 | tf_op jit(solution)/shard_map/ppermute | solution.py:28
  81.9 7.4 %collective-permute-start.9 = (bf16[2,288,128]{2,1,0:T(8,128)(2,1)}, bf16[2,288,128]{2,1,0:T(8,128)(2,1)S(1)}, u32[]{:S(2)}, u32[]{:S(2)}) collective-permute-start(bf16[2,288,128]{2,1,0:T(8,128)(2,1)} %get-tuple-element.49), channel_id=1, source_target_pairs={{0,8},{8,16},{16,24},{24,32},{32,40},{40,48},{48,56},{56,64},{64,7... | collective-permute-start | bytes 442376 | tf_op jit(solution)/shard_map/ppermute | solution.py:28
  95.0 14.4 %collective-permute-start.12 = (bf16[2,288,128]{2,1,0:T(8,128)(2,1)S(1)}, bf16[2,288,128]{2,1,0:T(8,128)(2,1)S(1)}, u32[]{:S(2)}, u32[]{:S(2)}) collective-permute-start(bf16[2,288,128]{2,1,0:T(8,128)(2,1)S(1)} %get-tuple-element.56), channel_id=1, source_target_pairs={{0,120},{8,0},{16,8},{24,16},{32,24},{40,32},{48,40},{56,48},{64,5... | collective-permute-start | bytes 442376 | tf_op jit(solution)/shard_map/ppermute | solution.py:28
  97.8 11.6 %collective-permute-start.13 = (bf16[2,288,128]{2,1,0:T(8,128)(2,1)S(1)}, bf16[2,288,128]{2,1,0:T(8,128)(2,1)S(1)}, u32[]{:S(2)}, u32[]{:S(2)}) collective-permute-start(bf16[2,288,128]{2,1,0:T(8,128)(2,1)S(1)} %get-tuple-element.57), channel_id=1, source_target_pairs={{0,8},{8,16},{16,24},{24,32},{32,40},{40,48},{48,56},{56,64},{64,7... | collective-permute-start | bytes 442376 | tf_op jit(solution)/shard_map/ppermute | solution.py:28
  97.8 6.2 %collective-permute-start.10 = (bf16[1,288,128]{2,1,0:T(8,128)(2,1)S(1)}, bf16[1,288,128]{2,1,0:T(8,128)(2,1)S(1)}, u32[]{:S(2)}, u32[]{:S(2)}) collective-permute-start(bf16[1,288,128]{2,1,0:T(8,128)(2,1)S(1)} %get-tuple-element.54), channel_id=1, source_target_pairs={{0,7},{1,0},{2,1},{3,2},{4,3},{5,4},{6,5},{7,6},{8,15},{9,8},{10,9... | collective-permute-start | bytes 221192 | tf_op jit(solution)/shard_map/ppermute | solution.py:28
  102.6 6.8 %collective-permute-start.11 = (bf16[1,288,128]{2,1,0:T(8,128)(2,1)S(1)}, bf16[1,288,128]{2,1,0:T(8,128)(2,1)S(1)}, u32[]{:S(2)}, u32[]{:S(2)}) collective-permute-start(bf16[1,288,128]{2,1,0:T(8,128)(2,1)S(1)} %get-tuple-element.55), channel_id=1, source_target_pairs={{0,1},{1,2},{2,3},{3,4},{4,5},{5,6},{6,7},{7,0},{8,9},{9,10},{10,1... | collective-permute-start | bytes 221192 | tf_op jit(solution)/shard_map/ppermute | solution.py:28
  111.9 23.5 %all-to-all-start.4 = ((bf16[128,24,128]{2,1,0:T(8,128)(2,1)}), bf16[128,24,128]{2,1,0:T(8,128)(2,1)S(1)}, u32[]{:S(2)}, u32[]{:S(2)}) async-start(bf16[128,24,128]{2,1,0:T(8,128)(2,1)} %broadcast_in_dim.19), calls=%async_computation.4 | async-start | bytes 1572864 | tf_op jit(solution)/shard_map/all_to_all | solution.py:33
  127.2 14.4 %collective-permute-start.16 = (bf16[2,288,128]{2,1,0:T(8,128)(2,1)}, bf16[2,288,128]{2,1,0:T(8,128)(2,1)S(1)}, u32[]{:S(2)}, u32[]{:S(2)}) collective-permute-start(bf16[2,288,128]{2,1,0:T(8,128)(2,1)} %get-tuple-element.64), channel_id=1, source_target_pairs={{0,120},{8,0},{16,8},{24,16},{32,24},{40,32},{48,40},{56,48},{64,5... | collective-permute-start | bytes 442376 | tf_op jit(solution)/shard_map/ppermute | solution.py:28
  128.6 13.0 %collective-permute-start.17 = (bf16[2,288,128]{2,1,0:T(8,128)(2,1)}, bf16[2,288,128]{2,1,0:T(8,128)(2,1)S(1)}, u32[]{:S(2)}, u32[]{:S(2)}) collective-permute-start(bf16[2,288,128]{2,1,0:T(8,128)(2,1)} %get-tuple-element.65), channel_id=1, source_target_pairs={{0,8},{8,16},{16,24},{24,32},{32,40},{40,48},{48,56},{56,64},{64,7... | collective-permute-start | bytes 442376 | tf_op jit(solution)/shard_map/ppermute | solution.py:28
  128.9 7.5 %collective-permute-start.14 = (bf16[1,288,128]{2,1,0:T(8,128)(2,1)}, bf16[1,288,128]{2,1,0:T(8,128)(2,1)S(1)}, u32[]{:S(2)}, u32[]{:S(2)}) collective-permute-start(bf16[1,288,128]{2,1,0:T(8,128)(2,1)} %get-tuple-element.62), channel_id=1, source_target_pairs={{0,7},{1,0},{2,1},{3,2},{4,3},{5,4},{6,5},{7,6},{8,15},{9,8},{10,9... | collective-permute-start | bytes 221192 | tf_op jit(solution)/shard_map/ppermute | solution.py:28
  134.7 6.8 %collective-permute-start.15 = (bf16[1,288,128]{2,1,0:T(8,128)(2,1)S(1)}, bf16[1,288,128]{2,1,0:T(8,128)(2,1)S(1)}, u32[]{:S(2)}, u32[]{:S(2)}) collective-permute-start(bf16[1,288,128]{2,1,0:T(8,128)(2,1)S(1)} %get-tuple-element.63), channel_id=1, source_target_pairs={{0,1},{1,2},{2,3},{3,4},{4,5},{5,6},{6,7},{7,0},{8,9},{9,10},{10,1... | collective-permute-start | bytes 221192 | tf_op jit(solution)/shard_map/ppermute | solution.py:28
  147.3 8.2 %collective-permute-start.19 = (bf16[2,288,128]{2,1,0:T(8,128)(2,1)S(1)}, bf16[2,288,128]{2,1,0:T(8,128)(2,1)S(1)}, u32[]{:S(2)}, u32[]{:S(2)}) collective-permute-start(bf16[2,288,128]{2,1,0:T(8,128)(2,1)S(1)} %get-tuple-element.69), channel_id=1, source_target_pairs={{0,120},{8,0},{16,8},{24,16},{32,24},{40,32},{48,40},{56,48},{64,5... | collective-permute-start | bytes 442376 | tf_op jit(solution)/shard_map/ppermute | solution.py:28
  150.7 4.8 %collective-permute-start.18 = (bf16[1,288,128]{2,1,0:T(8,128)(2,1)S(1)}, bf16[1,288,128]{2,1,0:T(8,128)(2,1)S(1)}, u32[]{:S(2)}, u32[]{:S(2)}) collective-permute-start(bf16[1,288,128]{2,1,0:T(8,128)(2,1)S(1)} %get-tuple-element.68), channel_id=1, source_target_pairs={{0,7},{1,0},{2,1},{3,2},{4,3},{5,4},{6,5},{7,6},{8,15},{9,8},{10,9... | collective-permute-start | bytes 221192 | tf_op jit(solution)/shard_map/ppermute | solution.py:28
  (14 other events, 137.9 us)
where the time goes:
time: 159 us; the launch traced here: 156 us
  starting transfers between devices  57.1 us (36%)
  Pallas kernels  35 us (22%)
  waiting for transfers between devices  30.6 us (19%)
  blocking collectives  14.6 us (9%)
  local copies, waits for them, and re-layouts  12.2 us (8%)
  matrix products  4.3 us (3%)
  other arithmetic  1.65 us (1%)
    ppermute x20, starting transfers between devices, shifted(): lax.ppermute(shard, axis, [(i, (i + by) % peers) for i in range(peers)])  35.4 us
    pallas_call x5, Pallas kernels, product_call(): pl.pallas_call(body, out_shape=outs, in_specs=[SMEM, HBM, HBM, *specs], o...  30.2 us
    ppermute x20, waiting for transfers between devices, shifted(): lax.ppermute(shard, axis, [(i, (i + by) % peers) for i in range(peers)])  27.4 us
    all_to_all x3, starting transfers between devices, copies_of_all(): lax.all_to_all(jnp.broadcast_to(shard[None], (peers, *shard.shape)), axis...  17.5 us
    all_to_all x1, blocking collectives, copies_of_all(): lax.all_to_all(jnp.broadcast_to(shard[None], (peers, *shard.shape)), axis...  14.6 us
    unnamed x37, local copies, waits for them, and re-layouts  6.36 us
    dot_general x2, matrix products, dot(): lax.dot_general(a, b, (contract, ((), ())), preferred_element_type=F32)  4.3 us
    all_to_all x1, starting transfers between devices, coarse_rows(): chosen = lax.all_to_all(chosen, 'sy', 0, 0, tiled=True)  4.19 us
  transfers between devices with their start and end apart: 24, of which 11 were waited for; matrix products, arithmetic and copies ran while one was open for 4% of the time, Pallas kernels for 14%

commit v1 on v0

--- a/solution.py
+++ b/solution.py
@@ -101,8 +101,7 @@
 
 
 def product_call(
-    body, flags, taut, wrinkle, others, specs, rows, extra_rows, more_out=(), more_scratch=(),
-    limit=PRODUCT_VMEM,
+    body, flags, taut, wrinkle, others, specs, rows, extra_rows, more_out=(), limit=PRODUCT_VMEM
 ):
     order = 4 * rows
     sent = rows + extra_rows
@@ -120,10 +119,9 @@
         in_specs=[SMEM, HBM, HBM, *specs],
         out_specs=[VMEM] * len(outs),
         scratch_shapes=[
-            pltpu.VMEM((2, order, LANES), BF16),
-            pltpu.VMEM((2, 2, order, order), BF16),
-            pltpu.SemaphoreType.DMA((2, 2, 2)),
-            *more_scratch,
+pltpu.VMEM((2, order, LANES), BF16),
+pltpu.VMEM((2, 2, order, order), BF16),
+pltpu.SemaphoreType.DMA((2, 2, 2)),
         ],
         compiler_params=pltpu.CompilerParams(vmem_limit_bytes=limit),
     )(flags, taut, wrinkle, *others)
@@ -265,14 +263,11 @@
     )(result, *incoming, lens, coupling, extra)
 
 
-def dual_body(flags, taut, wrinkle, source, result, east, west, south, north,
-              vectors, held, arrived, loaded):
+def dual_body(flags, taut, wrinkle, vectors, result, east, west, south, north,
+              unused, held, arrived):
     rows = result.shape[2]
-    own = pltpu.make_async_copy(source, vectors, loaded)
-    own.start()
     copies = loads_of(taut, wrinkle, held, arrived)
     start_loads(copies)
-    own.wait()
     product(copies, flags, held, vectors, result, (east, west, south, north), rows)
 
 
@@ -343,7 +338,8 @@
     cols_of = lax.axis_size("sy")
     per = 2 * CORNERS
     row_index = lax.axis_index("sx")
-    row_maps = copies_of_all(corner_map.reshape(1, per), "sy").reshape(cols_of * per)
+    tile_of = jnp.pad(corner_map.reshape(1, per), ((0, 7), (0, LANES - per)))
+    row_maps = copies_of_all(tile_of, "sy")[:, 0, :per].reshape(cols_of * per)
     codes = jnp.concatenate([row_maps // 32, row_maps % 32]).astype(BF16)
     code_rows = codes.shape[0] // LANES
     tile = jnp.pad(coarse_inverse, ((0, 0), (0, LANES - col_count)))
@@ -438,8 +434,7 @@
             terms, vectors, kept = terms_call(1, result, incoming, lens, coupling, kept)
         everyone = copies_of_all(terms, ("sx", "sy")).reshape(-1, LANES)
         result, *outgoing = product_call(
-            dual_body, flags, dual_taut, dual_wrinkle, (vectors,), [HBM],
-            rows, 0, (), [pltpu.SemaphoreType.DMA],
+            dual_body, flags, dual_taut, dual_wrinkle, (vectors,), [VMEM], rows, 0
         )
         incoming = exchanged(outgoing)
         base = correction_call(everyone, select, paired, start, lens)

time: 159 us -> 157 us (0.987)
    broadcast_in_dim x5 -> x4, local copies, waits for them, and re-layouts: 3.61 us -> 2.83 us  [copies_of_all(): jnp.broadcast_to(shard[None], (peers, *shard.shape))]
where the time goes in v1:
time: 157 us; the launch traced here: 155 us
  starting transfers between devices  57.2 us (36%)
  Pallas kernels  34.8 us (22%)
  waiting for transfers between devices  30.5 us (19%)
  blocking collectives  14.7 us (9%)
  local copies, waits for them, and re-layouts  11.7 us (7%)
  matrix products  4.29 us (3%)
    ppermute x20, starting transfers between devices, shifted(): lax.ppermute(shard, axis, [(i, (i + by) % peers) for i in range(peers)])  35.5 us
    pallas_call x5, Pallas kernels, product_call(): pl.pallas_call(body, out_shape=outs, in_specs=[SMEM, HBM, HBM, *specs], o...  30 us
    ppermute x20, waiting for transfers between devices, shifted(): lax.ppermute(shard, axis, [(i, (i + by) % peers) for i in range(peers)])  27.3 us
    all_to_all x3, starting transfers between devices, copies_of_all(): lax.all_to_all(jnp.broadcast_to(shard[None], (peers, *shard.shape)), axis...  17.5 us
    all_to_all x1, blocking collectives, copies_of_all(): lax.all_to_all(jnp.broadcast_to(shard[None], (peers, *shard.shape)), axis...  14.7 us
    unnamed x37, local copies, waits for them, and re-layouts  6.36 us
    dot_general x2, matrix products, dot(): lax.dot_general(a, b, (contract, ((), ())), preferred_element_type=F32)  4.29 us
    all_to_all x1, starting transfers between devices, coarse_rows(): chosen = lax.all_to_all(chosen, 'sy', 0, 0, tiled=True)  4.2 us
  transfers between devices with their start and end apart: 24, of which 11 were waited for; matrix products, arithmetic and copies ran while one was open for 4% of the time, Pallas kernels for 14%

profile of v1, /device:TPU:1, one launch (start us, length us, event | category | flops | bytes accessed | tf_op | source)
XLA Modules:
  0.0 155.1 jit_solution(2446127519536239282)
XLA Ops:
  1.4 14.7 %all_to_all.25 = s32[8,8,128]{2,1,0:T(8,128)S(1)} all-to-all(s32[8,8,128]{2,1,0:T(8,128)S(1)} %broadcast_in_dim.13), channel_id=1, replica_groups=mesh['sx'=16,'sy'=8] {'sy'}, dimensions={0} | all-to-all | bytes 65536 | tf_op jit(solution)/shard_map/all_to_all | solution.py:33
  17.8 6.7 %all-to-all-start.2 = ((bf16[16,64,128]{2,1,0:T(8,128)(2,1)}), bf16[16,64,128]{2,1,0:T(8,128)(2,1)S(1)}, u32[]{:S(2)}, u32[]{:S(2)}) async-start(bf16[16,64,128]{2,1,0:T(8,128)(2,1)} %broadcast_in_dim.14), calls=%async_computation.2 | async-start | bytes 524288 | tf_op jit(solution)/shard_map/all_to_all | solution.py:33
  29.4 2.4 %all-to-all-done.2 = bf16[16,64,128]{2,1,0:T(8,128)(2,1)S(1)} async-done(((bf16[16,64,128]{2,1,0:T(8,128)(2,1)}), bf16[16,64,128]{2,1,0:T(8,128)(2,1)S(1)}, u32[]{:S(2)}, u32[]{:S(2)}) %all-to-all-start.2) | async-done | bytes 262176 | tf_op jit(solution)/shard_map/all_to_all | solution.py:33
  34.1 4.2 %all-to-all-start.3 = ((bf16[8,128,128]{1,2,0:T(8,128)(2,1)}), bf16[8,128,128]{1,2,0:T(8,128)(2,1)}, u32[]{:S(2)}, u32[]{:S(2)}) async-start(bf16[8,128,128]{1,2,0:T(8,128)(2,1)} %copy.18), calls=%async_computation.3 | async-start | bytes 524288 | tf_op jit(solution)/shard_map/all_to_all | solution.py:371
  38.6 5.8 %shard_map.114 = (f32[2,4,288,128]{3,2,1,0:T(8,128)S(1)}, bf16[1,336,128]{2,1,0:T(8,128)(2,1)S(1)}, bf16[1,336,128]{2,1,0:T(8,128)(2,1)S(1)}, bf16[2,336,128]{2,...) custom-call(s32[2]{0:T(128)S(1)} %bitcast.70, ...), custom_call_target="tpu_custom_call" | custom-call | tf_op jit(solution)/shard_map/pallas_call | solution.py:116
  46.2 5.2 %collective-permute-start.2 = (bf16[1,336,128]{2,1,0:T(8,128)(2,1)S(1)}, bf16[1,336,128]{2,1,0:T(8,128)(2,1)S(1)}, u32[]{:S(2)}, u32[]{:S(2)}) collective-permute-start(bf16[1,336,128]{2,1,0:T(8,128)(2,1)S(1)} %get-tuple-element.39), channel_id=1, source_target_pairs={{0,7},{1,0},{2,1},{3,2},{4,3},{5,4},{6,5},{7,6},{8,15},{9,8},{10,9... | collective-permute-start | bytes 258056 | tf_op jit(solution)/shard_map/ppermute | solution.py:28
  51.4 4.3 %collective-permute-done.2.east = bf16[1,336,128]{2,1,0:T(8,128)(2,1)S(1)} collective-permute-done((bf16[1,336,128]{2,1,0:T(8,128)(2,1)S(1)}, bf16[1,336,128]{2,1,0:T(8,128)(2,1)S(1)}, u32[]{:S(2)}, u32[]{:S(2)}) %collective-permute-start.2) | collective-permute-done | bytes 86048 | tf_op jit(solution)/shard_map/ppermute | solution.py:28
  55.8 3.9 %collective-permute-done.3.west = bf16[1,336,128]{2,1,0:T(8,128)(2,1)S(1)} collective-permute-done((bf16[1,336,128]{2,1,0:T(8,128)(2,1)S(1)}, bf16[1,336,128]{2,1,0:T(8,128)(2,1)S(1)}, u32[]{:S(2)}, u32[]{:S(2)}) %collective-permute-start.3) | collective-permute-done | bytes 86048 | tf_op jit(solution)/shard_map/ppermute | solution.py:28
  62.2 4.2 %all-to-all-start = ((bf16[128,24,128]{2,1,0:T(8,128)(2,1)}), bf16[128,24,128]{2,1,0:T(8,128)(2,1)S(1)}, u32[]{:S(2)}, u32[]{:S(2)}) async-start(bf16[128,24,128]{2,1,0:T(8,128)(2,1)} %broadcast_in_dim.12), calls=%async_computation | async-start | bytes 1572864 | tf_op jit(solution)/shard_map/all_to_all | solution.py:33
  66.8 6.4 %shard_map.116 = (f32[2,4,288,128]{3,2,1,0:T(8,128)S(1)}, bf16[1,288,128]{2,1,0:T(8,128)(2,1)}, bf16[1,288,128]{2,1,0:T(8,128)(2,1)}, bf16[2,288,128]{2,1,0:T(8,128)(2,1)}, bf16[2,288,128]{2,1,0:T(8,128)(2,1)}) custom-call(s32[2]{0:T(128)S(1)} %bitcast.71, bf16[1,2,1152,1152]{3,2,1,0:T(8,128)(2,1)} %taut.8, bf16[1,2,1152,1152]{3,2,1,0:T(8,128)(2,1)} %wrinkle.8, ...), custom_call_target="tpu_custom_call" | custom-call | tf_op jit(solution)/shard_map/pallas_call | solution.py:116
  74.2 5.8 %collective-permute-start.6 = (bf16[1,288,128]{2,1,0:T(8,128)(2,1)}, bf16[1,288,128]{2,1,0:T(8,128)(2,1)S(1)}, u32[]{:S(2)}, u32[]{:S(2)}) collective-permute-start(bf16[1,288,128]{2,1,0:T(8,128)(2,1)} %get-tuple-element.46), channel_id=1, source_target_pairs={{0,7},{1,0},{2,1},{3,2},{4,3},{5,4},{6,5},{7,6},{8,15},{9,8},{10,9... | collective-permute-start | bytes 221192 | tf_op jit(solution)/shard_map/ppermute | solution.py:28
  81.8 3.5 %fusion.3.select = bf16[128,3072]{1,0:T(8,128)(2,1)S(1)} fusion(bf16[128,1024]{0,1:T(8,128)(2,1)} %bitcast.28, s32[3072]{0:T(1024)S(1)} %fusion.9), kind=kOutput, calls=%fused_computation.5 | convolution fusion | flops 808845312 | bytes 1060864 | tf_op jit(solution)/shard_map/dot_general | solution.py:48
  88.1 5.7 %shard_map.118 = (f32[2,4,288,128]{3,2,1,0:T(8,128)S(1)}, bf16[1,288,128]{2,1,0:T(8,128)(2,1)S(1)}, bf16[1,288,128]{2,1,0:T(8,128)(2,1)S(1)}, bf16[2,288,128]{2,1,0:T(8,128)(2,1)S(1)}, bf16[2,288,128]{2,1,0:T(8,128)(2,1)S(1)}) custom-call(s32[2]{0:T(128)S(1)} %bitcast.72, bf16[1,2,1152,1152]{3,2,1,0:T(8,128)(2,1)} %taut.9, ...), custom_call_target="tpu_custom_call" | custom-call | tf_op jit(solution)/shard_map/pallas_call | solution.py:116
  93.8 2.8 %collective-permute-start.12 = (bf16[2,288,128]{2,1,0:T(8,128)(2,1)S(1)}, bf16[2,288,128]{2,1,0:T(8,128)(2,1)S(1)}, u32[]{:S(2)}, u32[]{:S(2)}) collective-permute-start(bf16[2,288,128]{2,1,0:T(8,128)(2,1)S(1)} %get-tuple-element.56), channel_id=1, source_target_pairs={{0,120},{8,0},{16,8},{24,16},{32,24},{40,32},{48,40},{56,48},{64,5... | collective-permute-start | bytes 442376 | tf_op jit(solution)/shard_map/ppermute | solution.py:28
  96.6 4.8 %collective-permute-start.10 = (bf16[1,288,128]{2,1,0:T(8,128)(2,1)S(1)}, bf16[1,288,128]{2,1,0:T(8,128)(2,1)S(1)}, u32[]{:S(2)}, u32[]{:S(2)}) collective-permute-start(bf16[1,288,128]{2,1,0:T(8,128)(2,1)S(1)} %get-tuple-element.54), channel_id=1, source_target_pairs={{0,7},{1,0},{2,1},{3,2},{4,3},{5,4},{6,5},{7,6},{8,15},{9,8},{10,9... | collective-permute-start | bytes 221192 | tf_op jit(solution)/shard_map/ppermute | solution.py:28
  101.4 1.4 collective-permute-done.10.east
  102.8 5.4 %collective-permute-done.11.west = bf16[1,288,128]{2,1,0:T(8,128)(2,1)S(1)} collective-permute-done((bf16[1,288,128]{2,1,0:T(8,128)(2,1)S(1)}, bf16[1,288,128]{2,1,0:T(8,128)(2,1)S(1)}, u32[]{:S(2)}, u32[]{:S(2)}) %collective-permute-start.11) | collective-permute-done | bytes 73760 | tf_op jit(solution)/shard_map/ppermute | solution.py:28
  110.7 6.6 %all-to-all-start.4 = ((bf16[128,24,128]{2,1,0:T(8,128)(2,1)}), bf16[128,24,128]{2,1,0:T(8,128)(2,1)S(1)}, u32[]{:S(2)}, u32[]{:S(2)}) async-start(bf16[128,24,128]{2,1,0:T(8,128)(2,1)} %broadcast_in_dim.16), calls=%async_computation.4 | async-start | bytes 1572864 | tf_op jit(solution)/shard_map/all_to_all | solution.py:33
  118.4 6.4 %shard_map.120 = (f32[2,4,288,128]{3,2,1,0:T(8,128)S(1)}, bf16[1,288,128]{2,1,0:T(8,128)(2,1)S(1)}, bf16[1,288,128]{2,1,0:T(8,128)(2,1)}, bf16[2,288,128]{2,1,0:T(8,128)(2,1)}, bf16[2,288,128]{2,1,0:T(8,128)(2,1)}) custom-call(s32[2]{0:T(128)S(1)} %bitcast.73, bf16[1,2,1152,1152]{3,2,1,0:T(8,128)(2,1)} %taut.8, bf16[1,2,1152,1152]{3,2,1,0:T(8,128)(2,1)} %wrinkle.8, ...), custom_call_target="tpu_custom_call" | custom-call | tf_op jit(solution)/shard_map/pallas_call | solution.py:116
  127.6 5.8 %collective-permute-start.14 = (bf16[1,288,128]{2,1,0:T(8,128)(2,1)}, bf16[1,288,128]{2,1,0:T(8,128)(2,1)S(1)}, u32[]{:S(2)}, u32[]{:S(2)}) collective-permute-start(bf16[1,288,128]{2,1,0:T(8,128)(2,1)} %get-tuple-element.62), channel_id=1, source_target_pairs={{0,7},{1,0},{2,1},{3,2},{4,3},{5,4},{6,5},{7,6},{8,15},{9,8},{10,9... | collective-permute-start | bytes 221192 | tf_op jit(solution)/shard_map/ppermute | solution.py:28
  135.2 5.1 %collective-permute-done.15.from_west = bf16[1,288,128]{2,1,0:T(8,128)(2,1)S(1)} collective-permute-done((bf16[1,288,128]{2,1,0:T(8,128)(2,1)S(1)}, bf16[1,288,128]{2,1,0:T(8,128)(2,1)S(1)}, u32[]{:S(2)}, u32[]{:S(2)}) %collective-permute-start.15) | collective-permute-done | bytes 73760 | tf_op jit(solution)/shard_map/ppermute | solution.py:28
  140.3 5.7 %shard_map.122 = (f32[2,4,288,128]{3,2,1,0:T(8,128)S(1)}, bf16[1,288,128]{2,1,0:T(8,128)(2,1)}, bf16[1,288,128]{2,1,0:T(8,128)(2,1)S(1)}, bf16[2,288,128]{2,1,0:T(8,128)(2,1)}, bf16[2,288,128]{2,1,0:T(8,128)(2,1)S(1)}) custom-call(s32[2]{0:T(128)S(1)} %bitcast.74, bf16[1,2,1152,1152]{3,2,1,0:T(8,128)(2,1)} %taut.9, bf16[1,2,1152,1152]{3,2,1,0:T(8,128)(2,1)} %wrinkle.9, ...), custom_call_target="tpu_custom_call" | custom-call | tf_op jit(solution)/shard_map/pallas_call | solution.py:116
  146.0 3.4 %collective-permute-start.19 = (bf16[2,288,128]{2,1,0:T(8,128)(2,1)S(1)}, bf16[2,288,128]{2,1,0:T(8,128)(2,1)S(1)}, u32[]{:S(2)}, u32[]{:S(2)}) collective-permute-start(bf16[2,288,128]{2,1,0:T(8,128)(2,1)S(1)} %get-tuple-element.69), channel_id=1, source_target_pairs={{0,120},{8,0},{16,8},{24,16},{32,24},{40,32},{48,40},{56,48},{64,5... | collective-permute-start | bytes 442376 | tf_op jit(solution)/shard_map/ppermute | solution.py:28
  149.4 4.8 %collective-permute-done.18.east = bf16[1,288,128]{2,1,0:T(8,128)(2,1)S(1)} collective-permute-done((bf16[1,288,128]{2,1,0:T(8,128)(2,1)S(1)}, bf16[1,288,128]{2,1,0:T(8,128)(2,1)S(1)}, u32[]{:S(2)}, u32[]{:S(2)}) %collective-permute-start.18) | collective-permute-done | bytes 73760 | tf_op jit(solution)/shard_map/ppermute | solution.py:28
  (110 shorter events, 29.0 us)
Async XLA Ops:
  17.8 13.9 %all-to-all-start.2 = ((bf16[16,64,128]{2,1,0:T(8,128)(2,1)}), bf16[16,64,128]{2,1,0:T(8,128)(2,1)S(1)}, u32[]{:S(2)}, u32[]{:S(2)}) async-start(bf16[16,64,128]{2,1,0:T(8,128)(2,1)} %broadcast_in_dim.14), calls=%async_computation.2 | async-start | bytes 524288 | tf_op jit(solution)/shard_map/all_to_all | solution.py:33
  27.0 11.5 %collective-permute-start = (bf16[1,304,128]{2,1,0:T(8,128)(2,1)S(1)}, bf16[1,304,128]{2,1,0:T(8,128)(2,1)S(1)}, u32[]{:S(2)}, u32[]{:S(2)}) collective-permute-start(bf16[1,304,128]{2,1,0:T(8,128)(2,1)S(1)} %get-tuple-element.36), channel_id=1, source_target_pairs={{0,1},{1,2},{2,3},{3,4},{4,5},{5,6},{6,7},{7,0},{8,9},{9,10},{10,1... | collective-permute-start | bytes 233480 | tf_op jit(solution)/shard_map/ppermute | solution.py:28
  28.1 10.5 %collective-permute-start.1 = (bf16[2,304,128]{2,1,0:T(8,128)(2,1)S(1)}, bf16[2,304,128]{2,1,0:T(8,128)(2,1)S(1)}, u32[]{:S(2)}, u32[]{:S(2)}) collective-permute-start(bf16[2,304,128]{2,1,0:T(8,128)(2,1)S(1)} %get-tuple-element.37), channel_id=1, source_target_pairs={{0,8},{8,16},{16,24},{24,32},{32,40},{40,48},{48,56},{56,64},{64,7... | collective-permute-start | bytes 466952 | tf_op jit(solution)/shard_map/ppermute | solution.py:28
  34.1 27.2 %all-to-all-start.3 = ((bf16[8,128,128]{1,2,0:T(8,128)(2,1)}), bf16[8,128,128]{1,2,0:T(8,128)(2,1)}, u32[]{:S(2)}, u32[]{:S(2)}) async-start(bf16[8,128,128]{1,2,0:T(8,128)(2,1)} %copy.18), calls=%async_computation.3 | async-start | bytes 524288 | tf_op jit(solution)/shard_map/all_to_all | solution.py:371
  44.4 15.3 %collective-permute-start.4 = (bf16[2,336,128]{2,1,0:T(8,128)(2,1)S(1)}, bf16[2,336,128]{2,1,0:T(8,128)(2,1)S(1)}, u32[]{:S(2)}, u32[]{:S(2)}) collective-permute-start(bf16[2,336,128]{2,1,0:T(8,128)(2,1)S(1)} %get-tuple-element.41), channel_id=1, source_target_pairs={{0,120},{8,0},{16,8},{24,16},{32,24},{40,32},{48,40},{56,48},{64,5... | collective-permute-start | bytes 516104 | tf_op jit(solution)/shard_map/ppermute | solution.py:28
  45.3 14.3 %collective-permute-start.5 = (bf16[2,336,128]{2,1,0:T(8,128)(2,1)S(1)}, bf16[2,336,128]{2,1,0:T(8,128)(2,1)S(1)}, u32[]{:S(2)}, u32[]{:S(2)}) collective-permute-start(bf16[2,336,128]{2,1,0:T(8,128)(2,1)S(1)} %get-tuple-element.42), channel_id=1, source_target_pairs={{0,8},{8,16},{16,24},{24,32},{32,40},{40,48},{48,56},{56,64},{64,7... | collective-permute-start | bytes 516104 | tf_op jit(solution)/shard_map/ppermute | solution.py:28
  46.2 9.6 %collective-permute-start.2 = (bf16[1,336,128]{2,1,0:T(8,128)(2,1)S(1)}, bf16[1,336,128]{2,1,0:T(8,128)(2,1)S(1)}, u32[]{:S(2)}, u32[]{:S(2)}) collective-permute-start(bf16[1,336,128]{2,1,0:T(8,128)(2,1)S(1)} %get-tuple-element.39), channel_id=1, source_target_pairs={{0,7},{1,0},{2,1},{3,2},{4,3},{5,4},{6,5},{7,6},{8,15},{9,8},{10,9... | collective-permute-start | bytes 258056 | tf_op jit(solution)/shard_map/ppermute | solution.py:28
  51.4 8.3 %collective-permute-start.3 = (bf16[1,336,128]{2,1,0:T(8,128)(2,1)S(1)}, bf16[1,336,128]{2,1,0:T(8,128)(2,1)S(1)}, u32[]{:S(2)}, u32[]{:S(2)}) collective-permute-start(bf16[1,336,128]{2,1,0:T(8,128)(2,1)S(1)} %get-tuple-element.40), channel_id=1, source_target_pairs={{0,1},{1,2},{2,3},{3,4},{4,5},{5,6},{6,7},{7,0},{8,9},{9,10},{10,1... | collective-permute-start | bytes 258056 | tf_op jit(solution)/shard_map/ppermute | solution.py:28
  62.2 23.0 %all-to-all-start = ((bf16[128,24,128]{2,1,0:T(8,128)(2,1)}), bf16[128,24,128]{2,1,0:T(8,128)(2,1)S(1)}, u32[]{:S(2)}, u32[]{:S(2)}) async-start(bf16[128,24,128]{2,1,0:T(8,128)(2,1)} %broadcast_in_dim.12), calls=%async_computation | async-start | bytes 1572864 | tf_op jit(solution)/shard_map/all_to_all | solution.py:33
  74.2 11.8 %collective-permute-start.6 = (bf16[1,288,128]{2,1,0:T(8,128)(2,1)}, bf16[1,288,128]{2,1,0:T(8,128)(2,1)S(1)}, u32[]{:S(2)}, u32[]{:S(2)}) collective-permute-start(bf16[1,288,128]{2,1,0:T(8,128)(2,1)} %get-tuple-element.46), channel_id=1, source_target_pairs={{0,7},{1,0},{2,1},{3,2},{4,3},{5,4},{6,5},{7,6},{8,15},{9,8},{10,9... | collective-permute-start | bytes 221192 | tf_op jit(solution)/shard_map/ppermute | solution.py:28
  80.0 7.0 %collective-permute-start.7 = (bf16[1,288,128]{2,1,0:T(8,128)(2,1)}, bf16[1,288,128]{2,1,0:T(8,128)(2,1)S(1)}, u32[]{:S(2)}, u32[]{:S(2)}) collective-permute-start(bf16[1,288,128]{2,1,0:T(8,128)(2,1)} %get-tuple-element.47), channel_id=1, source_target_pairs={{0,1},{1,2},{2,3},{3,4},{4,5},{5,6},{6,7},{7,0},{8,9},{9,10},{10,1... | collective-permute-start | bytes 221192 | tf_op jit(solution)/shard_map/ppermute | solution.py:28
  80.0 8.1 %collective-permute-start.8 = (bf16[2,288,128]{2,1,0:T(8,128)(2,1)}, bf16[2,288,128]{2,1,0:T(8,128)(2,1)S(1)}, u32[]{:S(2)}, u32[]{:S(2)}) collective-permute-start(bf16[2,288,128]{2,1,0:T(8,128)(2,1)} %get-tuple-element.48), channel_id=1, source_target_pairs={{0,120},{8,0},{16,8},{24,16},{32,24},{40,32},{48,40},{56,48},{64,5... | collective-permute-start | bytes 442376 | tf_op jit(solution)/shard_map/ppermute | solution.py:28
  80.7 7.4 %collective-permute-start.9 = (bf16[2,288,128]{2,1,0:T(8,128)(2,1)}, bf16[2,288,128]{2,1,0:T(8,128)(2,1)S(1)}, u32[]{:S(2)}, u32[]{:S(2)}) collective-permute-start(bf16[2,288,128]{2,1,0:T(8,128)(2,1)} %get-tuple-element.49), channel_id=1, source_target_pairs={{0,8},{8,16},{16,24},{24,32},{32,40},{40,48},{48,56},{56,64},{64,7... | collective-permute-start | bytes 442376 | tf_op jit(solution)/shard_map/ppermute | solution.py:28
  93.8 14.4 %collective-permute-start.12 = (bf16[2,288,128]{2,1,0:T(8,128)(2,1)S(1)}, bf16[2,288,128]{2,1,0:T(8,128)(2,1)S(1)}, u32[]{:S(2)}, u32[]{:S(2)}) collective-permute-start(bf16[2,288,128]{2,1,0:T(8,128)(2,1)S(1)} %get-tuple-element.56), channel_id=1, source_target_pairs={{0,120},{8,0},{16,8},{24,16},{32,24},{40,32},{48,40},{56,48},{64,5... | collective-permute-start | bytes 442376 | tf_op jit(solution)/shard_map/ppermute | solution.py:28
  96.6 11.6 %collective-permute-start.13 = (bf16[2,288,128]{2,1,0:T(8,128)(2,1)S(1)}, bf16[2,288,128]{2,1,0:T(8,128)(2,1)S(1)}, u32[]{:S(2)}, u32[]{:S(2)}) collective-permute-start(bf16[2,288,128]{2,1,0:T(8,128)(2,1)S(1)} %get-tuple-element.57), channel_id=1, source_target_pairs={{0,8},{8,16},{16,24},{24,32},{32,40},{40,48},{48,56},{56,64},{64,7... | collective-permute-start | bytes 442376 | tf_op jit(solution)/shard_map/ppermute | solution.py:28
  96.6 6.2 %collective-permute-start.10 = (bf16[1,288,128]{2,1,0:T(8,128)(2,1)S(1)}, bf16[1,288,128]{2,1,0:T(8,128)(2,1)S(1)}, u32[]{:S(2)}, u32[]{:S(2)}) collective-permute-start(bf16[1,288,128]{2,1,0:T(8,128)(2,1)S(1)} %get-tuple-element.54), channel_id=1, source_target_pairs={{0,7},{1,0},{2,1},{3,2},{4,3},{5,4},{6,5},{7,6},{8,15},{9,8},{10,9... | collective-permute-start | bytes 221192 | tf_op jit(solution)/shard_map/ppermute | solution.py:28
  101.4 6.8 %collective-permute-start.11 = (bf16[1,288,128]{2,1,0:T(8,128)(2,1)S(1)}, bf16[1,288,128]{2,1,0:T(8,128)(2,1)S(1)}, u32[]{:S(2)}, u32[]{:S(2)}) collective-permute-start(bf16[1,288,128]{2,1,0:T(8,128)(2,1)S(1)} %get-tuple-element.55), channel_id=1, source_target_pairs={{0,1},{1,2},{2,3},{3,4},{4,5},{5,6},{6,7},{7,0},{8,9},{9,10},{10,1... | collective-permute-start | bytes 221192 | tf_op jit(solution)/shard_map/ppermute | solution.py:28
  110.7 23.5 %all-to-all-start.4 = ((bf16[128,24,128]{2,1,0:T(8,128)(2,1)}), bf16[128,24,128]{2,1,0:T(8,128)(2,1)S(1)}, u32[]{:S(2)}, u32[]{:S(2)}) async-start(bf16[128,24,128]{2,1,0:T(8,128)(2,1)} %broadcast_in_dim.16), calls=%async_computation.4 | async-start | bytes 1572864 | tf_op jit(solution)/shard_map/all_to_all | solution.py:33
  125.9 14.4 %collective-permute-start.16 = (bf16[2,288,128]{2,1,0:T(8,128)(2,1)}, bf16[2,288,128]{2,1,0:T(8,128)(2,1)S(1)}, u32[]{:S(2)}, u32[]{:S(2)}) collective-permute-start(bf16[2,288,128]{2,1,0:T(8,128)(2,1)} %get-tuple-element.64), channel_id=1, source_target_pairs={{0,120},{8,0},{16,8},{24,16},{32,24},{40,32},{48,40},{56,48},{64,5... | collective-permute-start | bytes 442376 | tf_op jit(solution)/shard_map/ppermute | solution.py:28
  127.1 13.2 %collective-permute-start.17 = (bf16[2,288,128]{2,1,0:T(8,128)(2,1)}, bf16[2,288,128]{2,1,0:T(8,128)(2,1)S(1)}, u32[]{:S(2)}, u32[]{:S(2)}) collective-permute-start(bf16[2,288,128]{2,1,0:T(8,128)(2,1)} %get-tuple-element.65), channel_id=1, source_target_pairs={{0,8},{8,16},{16,24},{24,32},{32,40},{40,48},{48,56},{56,64},{64,7... | collective-permute-start | bytes 442376 | tf_op jit(solution)/shard_map/ppermute | solution.py:28
  127.6 7.5 %collective-permute-start.14 = (bf16[1,288,128]{2,1,0:T(8,128)(2,1)}, bf16[1,288,128]{2,1,0:T(8,128)(2,1)S(1)}, u32[]{:S(2)}, u32[]{:S(2)}) collective-permute-start(bf16[1,288,128]{2,1,0:T(8,128)(2,1)} %get-tuple-element.62), channel_id=1, source_target_pairs={{0,7},{1,0},{2,1},{3,2},{4,3},{5,4},{6,5},{7,6},{8,15},{9,8},{10,9... | collective-permute-start | bytes 221192 | tf_op jit(solution)/shard_map/ppermute | solution.py:28
  133.4 6.8 %collective-permute-start.15 = (bf16[1,288,128]{2,1,0:T(8,128)(2,1)S(1)}, bf16[1,288,128]{2,1,0:T(8,128)(2,1)S(1)}, u32[]{:S(2)}, u32[]{:S(2)}) collective-permute-start(bf16[1,288,128]{2,1,0:T(8,128)(2,1)S(1)} %get-tuple-element.63), channel_id=1, source_target_pairs={{0,1},{1,2},{2,3},{3,4},{4,5},{5,6},{6,7},{7,0},{8,9},{9,10},{10,1... | collective-permute-start | bytes 221192 | tf_op jit(solution)/shard_map/ppermute | solution.py:28
  146.0 8.2 %collective-permute-start.19 = (bf16[2,288,128]{2,1,0:T(8,128)(2,1)S(1)}, bf16[2,288,128]{2,1,0:T(8,128)(2,1)S(1)}, u32[]{:S(2)}, u32[]{:S(2)}) collective-permute-start(bf16[2,288,128]{2,1,0:T(8,128)(2,1)S(1)} %get-tuple-element.69), channel_id=1, source_target_pairs={{0,120},{8,0},{16,8},{24,16},{32,24},{40,32},{48,40},{56,48},{64,5... | collective-permute-start | bytes 442376 | tf_op jit(solution)/shard_map/ppermute | solution.py:28
  149.4 4.8 %collective-permute-start.18 = (bf16[1,288,128]{2,1,0:T(8,128)(2,1)S(1)}, bf16[1,288,128]{2,1,0:T(8,128)(2,1)S(1)}, u32[]{:S(2)}, u32[]{:S(2)}) collective-permute-start(bf16[1,288,128]{2,1,0:T(8,128)(2,1)S(1)} %get-tuple-element.68), channel_id=1, source_target_pairs={{0,7},{1,0},{2,1},{3,2},{4,3},{5,4},{6,5},{7,6},{8,15},{9,8},{10,9... | collective-permute-start | bytes 221192 | tf_op jit(solution)/shard_map/ppermute | solution.py:28
  (14 other events, 136.8 us)
